TPU v7x, 32 devices: a whole 2x2x4 slice. The times are simulated.
32 devices in a mesh: blk: 8 (over z, y), rep: 4 (over x, core).
Axes of the slice: x: 2, y: 2, z: 4, core: 2. Of those that a mesh axis runs over, the one named last changes fastest.
Arguments:
- features: bfloat16 [8192, 256], P(('blk', 'rep')), may hold values from -6 to 6
- tiles: bfloat16 [8, 64, 128, 128], P('blk', 'rep'), may hold values from -0.25 to 0.25
- tile_rows: int32 [8, 64], P('blk', 'rep'), may hold values from 0 to 7
- tile_cols: int32 [8, 64], P('blk', 'rep'), may hold values from 0 to 15
- counts: int32 [8, 4], P('blk', 'rep'), may hold values from 4 to 16
- weight: bfloat16 [256, 256], replicated, may hold values from -0.375 to 0.375
- bias: float32 [256], replicated, may hold values from -3 to 3
- cotangent: bfloat16 [8192, 256], P(('blk', 'rep')), may hold values from -6 to 6
Outputs:
- activations: bfloat16 [8192, 256], P(('blk', 'rep'))
- feature_grad: bfloat16 [8192, 256], P(('blk', 'rep'))
- weight_grad: float32 [256, 256], replicated
- bias_grad: float32 [256], replicated
All inputs are finite; a program needn't handle non-finite values.
Results may differ from a plain program's by a relative error of at most 0.006.
Values may be sent and summed in bfloat16 or wider, within the bound.
A program may use at most 64 MiB of HBM per device.

v0:
```python
import jax
import jax.numpy as jnp
from jax import lax
from jax.sharding import PartitionSpec as P


def shifted(block, axis, distance):
    devices = range(lax.axis_size(axis))
    route = [((i - distance) % len(devices), i) for i in devices]
    return lax.ppermute(block, axis, route)


def per_device(features, tiles, tile_rows, tile_cols, counts, weight, bias, cotangent):
    highest = lax.Precision.HIGHEST
    tile_size = tiles.shape[2]
    slot_count = tiles.shape[1]
    feat_width = features.shape[1]
    own_rows = features.shape[0]
    own_tiles = own_rows // tile_size
    rep_count = lax.axis_size("rep")
    blk_count = lax.axis_size("blk")
    slot_tiles = tiles[0]
    row_index = tile_rows[0]
    col_index = tile_cols[0]
    slot_live = (jnp.arange(slot_count, dtype=jnp.int32) < counts[0, 0]).astype(jnp.float32)
    wanted = col_index[:, None] * tile_size + jnp.arange(tile_size, dtype=jnp.int32)[None, :]
    piece = lax.all_gather(features, "blk", axis=0, tiled=True)
    piece_count = piece.shape[0]
    inside = (wanted >= 0) & (wanted < piece_count)
    clipped = jnp.clip(wanted, 0, piece_count - 1)
    taken = jnp.take(piece, clipped.reshape(-1), axis=0).reshape(slot_count, tile_size, feat_width)
    selected = jnp.where(inside[:, :, None], taken, jnp.zeros((), jnp.bfloat16))
    partial_value = jnp.einsum(
        "sij,sjf->sif", slot_tiles, selected, preferred_element_type=jnp.float32
    )
    row_onehot = (
        row_index[:, None] == jnp.arange(rep_count * own_tiles, dtype=jnp.int32)[None, :]
    ).astype(jnp.float32) * slot_live[:, None]
    summed = jnp.einsum("st,sif->tif", row_onehot, partial_value, precision=highest)
    aggregate = lax.psum_scatter(
        summed.reshape(rep_count * own_rows, feat_width), "rep", scatter_dimension=0, tiled=True
    ).astype(jnp.bfloat16)
    pre_act = jnp.dot(aggregate, weight, preferred_element_type=jnp.float32) + bias[None, :]
    logistic = jax.nn.sigmoid(pre_act)
    activations = (pre_act * logistic).astype(jnp.bfloat16)
    act_grad = (
        cotangent.astype(jnp.float32) * logistic * (1.0 + pre_act * (1.0 - logistic))
    ).astype(jnp.bfloat16)
    local_weight = jnp.dot(aggregate.T, act_grad, preferred_element_type=jnp.float32)
    local_bias = jnp.sum(act_grad.astype(jnp.float32), axis=0)
    weight_grad, bias_grad = lax.psum((local_weight, local_bias), ("blk", "rep"))
    scale_factor = 1.0 / (blk_count * rep_count)
    weight_grad = weight_grad * scale_factor
    bias_grad = bias_grad * scale_factor
    agg_grad = jnp.dot(act_grad, weight.T, preferred_element_type=jnp.float32).astype(jnp.bfloat16)
    gathered = lax.all_gather(agg_grad, "rep", axis=0, tiled=True).reshape(
        rep_count * own_tiles, tile_size, feat_width
    )
    chosen = jnp.take(gathered, row_index, axis=0)
    contribution = (
        jnp.einsum("sij,sif->sjf", slot_tiles, chosen, preferred_element_type=jnp.float32)
        * slot_live[:, None, None]
    )

    def column_terms(first_row, row_count):
        targets = first_row // tile_size + jnp.arange(row_count // tile_size, dtype=jnp.int32)
        col_onehot = (col_index[:, None] == targets[None, :]).astype(jnp.float32)
        placed = jnp.einsum("sp,sjf->pjf", col_onehot, contribution, precision=highest)
        return placed.reshape(row_count, feat_width)

    own_block = lax.axis_index("blk")

    def travel_step(step_index, travelling):
        source_block = (own_block - step_index) % blk_count
        travelling = travelling + column_terms(source_block * own_rows, own_rows)
        return shifted(travelling, "blk", 1)

    feature_sum = lax.fori_loop(
        0, blk_count, travel_step, jnp.zeros((own_rows, feat_width), jnp.float32)
    )
    feature_grad = feature_sum.astype(jnp.bfloat16)
    return (activations, feature_grad, weight_grad, bias_grad)


def solution(mesh):
    in_specs = (
        P(("blk", "rep"), None),
        P("blk", "rep", None, None),
        P("blk", "rep"),
        P("blk", "rep"),
        P("blk", "rep"),
        P(),
        P(),
        P(("blk", "rep"), None),
    )
    out_specs = (P(("blk", "rep"), None), P(("blk", "rep"), None), P(), P())
    return jax.shard_map(
        per_device, mesh=mesh, in_specs=in_specs, out_specs=out_specs, check_vma=False
    )
```

profile of v0, /device:TPU:10, one launch (start us, length us, event | category | flops | bytes accessed | tf_op | source)
XLA Modules:
  0.0 242.8 jit_solution(17766153802447288838)
XLA Ops:
  9.5 40.9 %all-gather.2.cloned.1.call-done = bf16[2048,256]{1,0:T(8,128)(2,1)} async-done(((bf16[256,256]{1,0:T(8,128)(2,1)}), bf16[2048,256]{1,0:T(8,128)(2,1)}) %all-gather.2.cloned.1.call-update) | async-done | bytes 1048592 | tf_op jit(solution)/shard_map/all_gather | solution.py:27
  50.4 9.8 %gather_fusion = bf16[2048,256]{1,0:T(8,128)(2,1)} fusion(bf16[2048,256]{1,0:T(8,128)(2,1)} %all-gather.2.cloned.1.call-done, s32[2048]{0:T(1024)S(1)} %broadcast_clamp_fusion), kind=kCustom, calls=%fused_computation | custom fusion | bytes 2105344 | tf_op jit(solution)/shard_map/jit(_take)/gather | solution.py:31
  60.2 2.3 fusion.8
  62.6 2.1 copy.18
  64.7 2.7 %fusion.5 = f32[8,128,256]{2,0,1:T(8,128)S(1)} fusion(f32[16,256,128]{1,0,2:T(8,128)} %copy.18, f32[16]{0:T(128)S(1)} %compare_convert_fusion, s32[16]{0:T(128)S(1)} %bitcast.53), kind=kOutput, calls=%fused_computation.9 | convolution fusion | flops 50331904 | bytes 3145856 | tf_op jit(solution)/shard_map/st,sif->tif/dot_general | solution.py:39
  67.4 1.3 copy.15
  68.8 23.8 %reduce-scatter.2.cloned.1.call-done = f32[256,256]{1,0:T(8,128)} async-done(((f32[1024,256]{1,0:T(8,128)}), f32[256,256]{1,0:T(8,128)}) %reduce-scatter.2.cloned.1.call-update) | async-done | bytes 262160 | tf_op jit(solution)/shard_map/reduce_scatter | solution.py:40
  92.7 2.0 convert_reduce_fusion
  94.9 0.9 fusion.19
  95.8 7.2 %all_gather.7 = bf16[1024,256]{1,0:T(8,128)(2,1)S(1)} all-gather(bf16[256,256]{1,0:T(8,128)(2,1)S(1)} %convolution_convert_fusion), channel_id=1, replica_groups=mesh['blk'=8,'rep'=4] {'rep'}, dimensions={0}, use_global_device_ids=true | all-gather | bytes 655360 | tf_op jit(solution)/shard_map/all_gather | solution.py:56
  103.6 1.9 multiply_bitcast_fusion
  105.5 2.3 copy.17
  107.8 78.2 %while.15 = (s32[]{:T(128)}, f32[256,256]{1,0:T(8,128)S(1)}, s32[1,16]{1,0:T(1,128)S(1)}, s32[]{:T(128)}, f32[16,128,256]{2,0,1:T(8,128)S(1)}, /*index=5*/s32[]{...) while((s32[]{:T(128)}, f32[256,256]{1,0:T(8,128)S(1)}, ...), condition=%wide.region_2.3_spmd, body=%wide.region_1.2_spmd.sunk | while | flops 12648512 | bytes 4719116 | solution.py:78
  107.9 0.8 fusion.46
  108.8 1.5 collective-permute-start
  110.3 8.3 %collective-permute-done = f32[256,256]{1,0:T(8,128)S(1)} collective-permute-done((f32[256,256]{1,0:T(8,128)S(1)}, f32[256,256]{1,0:T(8,128)S(1)}, u32[]{:S(2)}, u32[]{:S(2)}) %collective-permute-start) | collective-permute-done | bytes 262176 | tf_op jit(solution)/shard_map/while/body/eval_jaxpr/ppermute | solution.py:10
  118.6 0.8 fusion.46
  120.0 8.6 %collective-permute-done = f32[256,256]{1,0:T(8,128)S(1)} collective-permute-done((f32[256,256]{1,0:T(8,128)S(1)}, f32[256,256]{1,0:T(8,128)S(1)}, u32[]{:S(2)}, u32[]{:S(2)}) %collective-permute-start) | collective-permute-done | bytes 262176 | tf_op jit(solution)/shard_map/while/body/eval_jaxpr/ppermute | solution.py:10
  128.5 0.8 fusion.46
  129.5 7.8 %collective-permute-done = f32[256,256]{1,0:T(8,128)S(1)} collective-permute-done((f32[256,256]{1,0:T(8,128)S(1)}, f32[256,256]{1,0:T(8,128)S(1)}, u32[]{:S(2)}, u32[]{:S(2)}) %collective-permute-start) | collective-permute-done | bytes 262176 | tf_op jit(solution)/shard_map/while/body/eval_jaxpr/ppermute | solution.py:10
  137.3 0.8 fusion.46
  138.3 7.8 %collective-permute-done = f32[256,256]{1,0:T(8,128)S(1)} collective-permute-done((f32[256,256]{1,0:T(8,128)S(1)}, f32[256,256]{1,0:T(8,128)S(1)}, u32[]{:S(2)}, u32[]{:S(2)}) %collective-permute-start) | collective-permute-done | bytes 262176 | tf_op jit(solution)/shard_map/while/body/eval_jaxpr/ppermute | solution.py:10
  146.1 0.8 fusion.46
  147.1 8.3 %collective-permute-done = f32[256,256]{1,0:T(8,128)S(1)} collective-permute-done((f32[256,256]{1,0:T(8,128)S(1)}, f32[256,256]{1,0:T(8,128)S(1)}, u32[]{:S(2)}, u32[]{:S(2)}) %collective-permute-start) | collective-permute-done | bytes 262176 | tf_op jit(solution)/shard_map/while/body/eval_jaxpr/ppermute | solution.py:10
  155.4 0.8 fusion.46
  156.4 9.1 %collective-permute-done = f32[256,256]{1,0:T(8,128)S(1)} collective-permute-done((f32[256,256]{1,0:T(8,128)S(1)}, f32[256,256]{1,0:T(8,128)S(1)}, u32[]{:S(2)}, u32[]{:S(2)}) %collective-permute-start) | collective-permute-done | bytes 262176 | tf_op jit(solution)/shard_map/while/body/eval_jaxpr/ppermute | solution.py:10
  165.5 0.8 fusion.46
  166.5 9.4 %collective-permute-done = f32[256,256]{1,0:T(8,128)S(1)} collective-permute-done((f32[256,256]{1,0:T(8,128)S(1)}, f32[256,256]{1,0:T(8,128)S(1)}, u32[]{:S(2)}, u32[]{:S(2)}) %collective-permute-start) | collective-permute-done | bytes 262176 | tf_op jit(solution)/shard_map/while/body/eval_jaxpr/ppermute | solution.py:10
  175.9 0.8 fusion.46
  176.8 9.1 %collective-permute-done = f32[256,256]{1,0:T(8,128)S(1)} collective-permute-done((f32[256,256]{1,0:T(8,128)S(1)}, f32[256,256]{1,0:T(8,128)S(1)}, u32[]{:S(2)}, u32[]{:S(2)}) %collective-permute-start) | collective-permute-done | bytes 262176 | tf_op jit(solution)/shard_map/while/body/eval_jaxpr/ppermute | solution.py:10
  186.7 47.3 %psum.15 = f32[256]{0:T(256)S(1)} all-reduce(f32[256]{0:T(256)S(1)} %get-tuple-element.160), channel_id=1, replica_groups=mesh['blk'=8,'rep'=4] {'blk','rep'}, use_global_device_ids=true, to_apply=%region_5.6 | all-reduce | flops 256 | bytes 2048 | tf_op jit(solution)/shard_map/psum | solution.py:51
  234.6 1.7 broadcast_multiply_fusion
  (66 shorter events, 5.1 us)
Async XLA Ops:
  7.2 53.1 %copy-start = (bf16[1,16,128,128]{3,2,1,0:T(8,128)(2,1)S(1)}, bf16[1,16,128,128]{3,2,1,0:T(8,128)(2,1)}, u32[]{:S(2)}) copy-start(bf16[1,16,128,128]{3,2,1,0:T(8,128)(2,1)} %param.11) | copy-start | bytes 1572868
  7.2 43.2 %all-gather.2.cloned.1.call-start = ((), (), s32[]{:S(2)}) async-start(), calls=%async_computation.1 | async-start | bytes 1179648 | tf_op jit(solution)/shard_map/all_gather | solution.py:27
  7.9 84.7 %reduce-scatter.2.cloned.1.call-start = ((), (), s32[]{:S(2)}) async-start(), calls=%async_computation.2 | async-start | bytes 1310720 | tf_op jit(solution)/shard_map/reduce_scatter | solution.py:40
  62.6 2.1 copy-start.4
  67.4 25.3 %copy-start.2 = (bf16[256,256]{1,0:T(8,128)(2,1)S(1)}, bf16[256,256]{1,0:T(8,128)(2,1)}, u32[]{:S(2)}) copy-start(bf16[256,256]{1,0:T(8,128)(2,1)} %param.15) | copy-start | bytes 393220
  67.4 25.3 %copy-start.5 = (bf16[256,256]{1,0:T(8,128)(2,1)S(1)}, bf16[256,256]{1,0:T(8,128)(2,1)}, u32[]{:S(2)}) copy-start(bf16[256,256]{1,0:T(8,128)(2,1)} %param.17) | copy-start | bytes 393220
  67.4 25.2 %copy-start.6 = (f32[256]{0:T(256)S(1)}, f32[256]{0:T(256)}, u32[]{:S(2)}) copy-start(f32[256]{0:T(256)} %param.16) | copy-start | bytes 3076
  68.7 165.8 %all-reduce.2.cloned.1.call-start = ((), (), s32[]{:S(2)}) async-start(), calls=%async_computation.3 | async-start | bytes 524288 | tf_op jit(solution)/shard_map/psum | solution.py:51
  92.6 2.2 copy-start.1
  105.5 2.3 copy-start.3
  108.8 9.8 %collective-permute-start = (f32[256,256]{1,0:T(8,128)S(1)}, f32[256,256]{1,0:T(8,128)S(1)}, u32[]{:S(2)}, u32[]{:S(2)}) collective-permute-start(f32[256,256]{1,0:T(8,128)S(1)} %bitcast_add_fusion.2), channel_id=1, source_target_pairs={{28,0},{0,4},{4,8},{8,12},{12,16},{16,20},{20,24},{24,28},{29,1},{... | collective-permute-start | bytes 786440 | tf_op jit(solution)/shard_map/while/body/eval_jaxpr/ppermute | solution.py:10
  119.5 9.0 %collective-permute-start = (f32[256,256]{1,0:T(8,128)S(1)}, f32[256,256]{1,0:T(8,128)S(1)}, u32[]{:S(2)}, u32[]{:S(2)}) collective-permute-start(f32[256,256]{1,0:T(8,128)S(1)} %bitcast_add_fusion.2), channel_id=1, source_target_pairs={{28,0},{0,4},{4,8},{8,12},{12,16},{16,20},{20,24},{24,28},{29,1},{... | collective-permute-start | bytes 786440 | tf_op jit(solution)/shard_map/while/body/eval_jaxpr/ppermute | solution.py:10
  129.4 7.9 %collective-permute-start = (f32[256,256]{1,0:T(8,128)S(1)}, f32[256,256]{1,0:T(8,128)S(1)}, u32[]{:S(2)}, u32[]{:S(2)}) collective-permute-start(f32[256,256]{1,0:T(8,128)S(1)} %bitcast_add_fusion.2), channel_id=1, source_target_pairs={{28,0},{0,4},{4,8},{8,12},{12,16},{16,20},{20,24},{24,28},{29,1},{... | collective-permute-start | bytes 786440 | tf_op jit(solution)/shard_map/while/body/eval_jaxpr/ppermute | solution.py:10
  138.2 7.9 %collective-permute-start = (f32[256,256]{1,0:T(8,128)S(1)}, f32[256,256]{1,0:T(8,128)S(1)}, u32[]{:S(2)}, u32[]{:S(2)}) collective-permute-start(f32[256,256]{1,0:T(8,128)S(1)} %bitcast_add_fusion.2), channel_id=1, source_target_pairs={{28,0},{0,4},{4,8},{8,12},{12,16},{16,20},{20,24},{24,28},{29,1},{... | collective-permute-start | bytes 786440 | tf_op jit(solution)/shard_map/while/body/eval_jaxpr/ppermute | solution.py:10
  147.0 8.4 %collective-permute-start = (f32[256,256]{1,0:T(8,128)S(1)}, f32[256,256]{1,0:T(8,128)S(1)}, u32[]{:S(2)}, u32[]{:S(2)}) collective-permute-start(f32[256,256]{1,0:T(8,128)S(1)} %bitcast_add_fusion.2), channel_id=1, source_target_pairs={{28,0},{0,4},{4,8},{8,12},{12,16},{16,20},{20,24},{24,28},{29,1},{... | collective-permute-start | bytes 786440 | tf_op jit(solution)/shard_map/while/body/eval_jaxpr/ppermute | solution.py:10
  156.3 9.2 %collective-permute-start = (f32[256,256]{1,0:T(8,128)S(1)}, f32[256,256]{1,0:T(8,128)S(1)}, u32[]{:S(2)}, u32[]{:S(2)}) collective-permute-start(f32[256,256]{1,0:T(8,128)S(1)} %bitcast_add_fusion.2), channel_id=1, source_target_pairs={{28,0},{0,4},{4,8},{8,12},{12,16},{16,20},{20,24},{24,28},{29,1},{... | collective-permute-start | bytes 786440 | tf_op jit(solution)/shard_map/while/body/eval_jaxpr/ppermute | solution.py:10
  166.4 9.5 %collective-permute-start = (f32[256,256]{1,0:T(8,128)S(1)}, f32[256,256]{1,0:T(8,128)S(1)}, u32[]{:S(2)}, u32[]{:S(2)}) collective-permute-start(f32[256,256]{1,0:T(8,128)S(1)} %bitcast_add_fusion.2), channel_id=1, source_target_pairs={{28,0},{0,4},{4,8},{8,12},{12,16},{16,20},{20,24},{24,28},{29,1},{... | collective-permute-start | bytes 786440 | tf_op jit(solution)/shard_map/while/body/eval_jaxpr/ppermute | solution.py:10
  176.8 9.2 %collective-permute-start = (f32[256,256]{1,0:T(8,128)S(1)}, f32[256,256]{1,0:T(8,128)S(1)}, u32[]{:S(2)}, u32[]{:S(2)}) collective-permute-start(f32[256,256]{1,0:T(8,128)S(1)} %bitcast_add_fusion.2), channel_id=1, source_target_pairs={{28,0},{0,4},{4,8},{8,12},{12,16},{16,20},{20,24},{24,28},{29,1},{... | collective-permute-start | bytes 786440 | tf_op jit(solution)/shard_map/while/body/eval_jaxpr/ppermute | solution.py:10
Sparse Core Ops, SparseCore 0:
  10.1 40.2 all-gather.1
  68.9 23.7 reduce-scatter.1
  98.7 131.8 all-reduce.1
where the time goes:
time: 243 us
  waiting for transfers between devices  134 us (55%)
  blocking collectives  54.5 us (22%)
  matrix products  16.7 us (7%)
  local copies, waits for them, and re-layouts  16.3 us (7%)
  between operations  14.6 us (6%)
  other arithmetic  4.1 us (2%)
  starting transfers between devices  2.45 us (1%)
    ppermute x8, waiting for transfers between devices, shifted(): return lax.ppermute(block, axis, route)  68.5 us
    psum x1, blocking collectives, per_device(): lax.psum((local_weight, local_bias), ('blk', 'rep'))  47.3 us
    all_gather x1, waiting for transfers between devices, per_device(): piece = lax.all_gather(features, 'blk', axis=0, tiled=True)  40.9 us
    reduce_scatter x1, waiting for transfers between devices, per_device(): lax.psum_scatter(summed.reshape(rep_count * own_rows, feat_width), 'rep',...  23.8 us
    gather x1, local copies, waits for them, and re-layouts, per_device(): jnp.take(piece, clipped.reshape(-1), axis=0)  9.83 us
    all_gather x1, blocking collectives, per_device(): lax.all_gather(agg_grad, 'rep', axis=0, tiled=True)  7.17 us
    dot_general x8, matrix products, column_terms(): jnp.einsum('sp,sjf->pjf', col_onehot, contribution, precision=highest)  6.58 us
  transfers between devices with their start and end apart: 11, of which 10 were waited for; matrix products, arithmetic and copies ran while one was open for 6% of the time, Pallas kernels for 0%

commit v1 on v0

--- a/solution.py
+++ b/solution.py
@@ -48,7 +48,7 @@
     ).astype(jnp.bfloat16)
     local_weight = jnp.dot(aggregate.T, act_grad, preferred_element_type=jnp.float32)
     local_bias = jnp.sum(act_grad.astype(jnp.float32), axis=0)
-    weight_grad, bias_grad = lax.psum((local_weight, local_bias), ("blk", "rep"))
+    weight_grad, bias_grad = lax.psum(lax.psum((local_weight, local_bias), "rep"), "blk")
     scale_factor = 1.0 / (blk_count * rep_count)
     weight_grad = weight_grad * scale_factor
     bias_grad = bias_grad * scale_factor

time: 243 us -> 253 us (1.041)
  the two profiles are of different devices: /device:TPU:10 before, /device:TPU:0 now
where the time goes in v1:
time: 253 us
  waiting for transfers between devices  169 us (67%)
  blocking collectives  29.5 us (12%)
  matrix products  16.7 us (7%)
  local copies, waits for them, and re-layouts  16.2 us (6%)
  between operations  14.6 us (6%)
  other arithmetic  4.11 us (2%)
    ppermute x8, waiting for transfers between devices, shifted(): return lax.ppermute(block, axis, route)  80.3 us
    all_gather x1, waiting for transfers between devices, per_device(): piece = lax.all_gather(features, 'blk', axis=0, tiled=True)  43.7 us
    reduce_scatter x1, waiting for transfers between devices, per_device(): lax.psum_scatter(summed.reshape(rep_count * own_rows, feat_width), 'rep',...  23.6 us
    psum x1, waiting for transfers between devices, per_device(): lax.psum((local_weight, local_bias), 'rep')  21 us
    psum x1, blocking collectives, per_device(): lax.psum(lax.psum((local_weight, local_bias), 'rep'), 'blk')  17.1 us
    gather x1, local copies, waits for them, and re-layouts, per_device(): jnp.take(piece, clipped.reshape(-1), axis=0)  9.81 us
    all_gather x1, blocking collectives, per_device(): lax.all_gather(agg_grad, 'rep', axis=0, tiled=True)  6.61 us
    dot_general x8, matrix products, column_terms(): jnp.einsum('sp,sjf->pjf', col_onehot, contribution, precision=highest)  6.58 us
  transfers between devices with their start and end apart: 12, of which 11 were waited for; matrix products, arithmetic and copies ran while one was open for 6% of the time, Pallas kernels for 0%

profile of v1, /device:TPU:0, one launch (start us, length us, event | category | flops | bytes accessed | tf_op | source)
XLA Modules:
  0.0 252.6 jit_solution(17024513736372025570)
XLA Ops:
  9.5 43.7 %all-gather.2.cloned.1.call-done = bf16[2048,256]{1,0:T(8,128)(2,1)} async-done(((bf16[256,256]{1,0:T(8,128)(2,1)}), bf16[2048,256]{1,0:T(8,128)(2,1)}) %all-gather.2.cloned.1.call-update) | async-done | bytes 1048592 | tf_op jit(solution)/shard_map/all_gather | solution.py:27
  53.1 9.8 %gather_fusion = bf16[2048,256]{1,0:T(8,128)(2,1)} fusion(bf16[2048,256]{1,0:T(8,128)(2,1)} %all-gather.2.cloned.1.call-done, s32[2048]{0:T(1024)S(1)} %broadcast_clamp_fusion), kind=kCustom, calls=%fused_computation | custom fusion | bytes 2105344 | tf_op jit(solution)/shard_map/jit(_take)/gather | solution.py:31
  63.0 2.3 fusion.8
  65.3 2.1 copy.18
  67.4 2.7 %fusion.5 = f32[8,128,256]{2,0,1:T(8,128)S(1)} fusion(f32[16,256,128]{1,0,2:T(8,128)} %copy.18, f32[16]{0:T(128)S(1)} %compare_convert_fusion, s32[16]{0:T(128)S(1)} %bitcast.53), kind=kOutput, calls=%fused_computation.9 | convolution fusion | flops 50331904 | bytes 3145856 | tf_op jit(solution)/shard_map/st,sif->tif/dot_general | solution.py:39
  70.1 1.3 copy.15
  71.5 23.6 %reduce-scatter.2.cloned.1.call-done = f32[256,256]{1,0:T(8,128)} async-done(((f32[1024,256]{1,0:T(8,128)}), f32[256,256]{1,0:T(8,128)}) %reduce-scatter.2.cloned.1.call-update) | async-done | bytes 262160 | tf_op jit(solution)/shard_map/reduce_scatter | solution.py:40
  95.1 2.0 convert_reduce_fusion
  97.3 0.9 fusion.19
  98.3 6.6 %all_gather.7 = bf16[1024,256]{1,0:T(8,128)(2,1)S(1)} all-gather(bf16[256,256]{1,0:T(8,128)(2,1)S(1)} %convolution_convert_fusion), channel_id=1, replica_groups=mesh['blk'=8,'rep'=4] {'rep'}, dimensions={0}, use_global_device_ids=true | all-gather | bytes 655360 | tf_op jit(solution)/shard_map/all_gather | solution.py:56
  105.6 1.9 multiply_bitcast_fusion
  107.5 2.3 copy.17
  109.7 21.0 %all-reduce.3.cloned.1.call-done = f32[256,256]{1,0:T(8,128)} async-done(((f32[256,256]{1,0:T(8,128)}), f32[256,256]{1,0:T(8,128)}) %all-reduce.3.cloned.1.call-update) | async-done | bytes 262160 | tf_op jit(solution)/shard_map/psum | solution.py:51
  130.8 89.6 %while.15 = (s32[]{:T(128)}, f32[256,256]{1,0:T(8,128)S(1)}, s32[1,16]{1,0:T(1,128)S(1)}, s32[]{:T(128)}, f32[16,128,256]{2,0,1:T(8,128)S(1)}, /*index=5*/s32[]{...) while((s32[]{:T(128)}, f32[256,256]{1,0:T(8,128)S(1)}, ...), condition=%wide.region_2.3_spmd, body=%wide.region_1.2_spmd.sunk | while | flops 12648512 | bytes 4719116 | solution.py:78
  131.7 1.5 collective-permute-start
  133.3 7.9 %collective-permute-done = f32[256,256]{1,0:T(8,128)S(1)} collective-permute-done((f32[256,256]{1,0:T(8,128)S(1)}, f32[256,256]{1,0:T(8,128)S(1)}, u32[]{:S(2)}, u32[]{:S(2)}) %collective-permute-start) | collective-permute-done | bytes 262176 | tf_op jit(solution)/shard_map/while/body/eval_jaxpr/ppermute | solution.py:10
  141.2 0.8 fusion.46
  142.2 10.6 %collective-permute-done = f32[256,256]{1,0:T(8,128)S(1)} collective-permute-done((f32[256,256]{1,0:T(8,128)S(1)}, f32[256,256]{1,0:T(8,128)S(1)}, u32[]{:S(2)}, u32[]{:S(2)}) %collective-permute-start) | collective-permute-done | bytes 262176 | tf_op jit(solution)/shard_map/while/body/eval_jaxpr/ppermute | solution.py:10
  152.7 0.8 fusion.46
  153.7 9.3 %collective-permute-done = f32[256,256]{1,0:T(8,128)S(1)} collective-permute-done((f32[256,256]{1,0:T(8,128)S(1)}, f32[256,256]{1,0:T(8,128)S(1)}, u32[]{:S(2)}, u32[]{:S(2)}) %collective-permute-start) | collective-permute-done | bytes 262176 | tf_op jit(solution)/shard_map/while/body/eval_jaxpr/ppermute | solution.py:10
  163.0 0.8 fusion.46
  164.0 9.1 %collective-permute-done = f32[256,256]{1,0:T(8,128)S(1)} collective-permute-done((f32[256,256]{1,0:T(8,128)S(1)}, f32[256,256]{1,0:T(8,128)S(1)}, u32[]{:S(2)}, u32[]{:S(2)}) %collective-permute-start) | collective-permute-done | bytes 262176 | tf_op jit(solution)/shard_map/while/body/eval_jaxpr/ppermute | solution.py:10
  173.1 0.8 fusion.46
  174.1 9.9 %collective-permute-done = f32[256,256]{1,0:T(8,128)S(1)} collective-permute-done((f32[256,256]{1,0:T(8,128)S(1)}, f32[256,256]{1,0:T(8,128)S(1)}, u32[]{:S(2)}, u32[]{:S(2)}) %collective-permute-start) | collective-permute-done | bytes 262176 | tf_op jit(solution)/shard_map/while/body/eval_jaxpr/ppermute | solution.py:10
  184.0 0.8 fusion.46
  185.0 10.4 %collective-permute-done = f32[256,256]{1,0:T(8,128)S(1)} collective-permute-done((f32[256,256]{1,0:T(8,128)S(1)}, f32[256,256]{1,0:T(8,128)S(1)}, u32[]{:S(2)}, u32[]{:S(2)}) %collective-permute-start) | collective-permute-done | bytes 262176 | tf_op jit(solution)/shard_map/while/body/eval_jaxpr/ppermute | solution.py:10
  196.4 13.9 %collective-permute-done = f32[256,256]{1,0:T(8,128)S(1)} collective-permute-done((f32[256,256]{1,0:T(8,128)S(1)}, f32[256,256]{1,0:T(8,128)S(1)}, u32[]{:S(2)}, u32[]{:S(2)}) %collective-permute-start) | collective-permute-done | bytes 262176 | tf_op jit(solution)/shard_map/while/body/eval_jaxpr/ppermute | solution.py:10
  210.3 0.8 fusion.46
  211.3 9.1 %collective-permute-done = f32[256,256]{1,0:T(8,128)S(1)} collective-permute-done((f32[256,256]{1,0:T(8,128)S(1)}, f32[256,256]{1,0:T(8,128)S(1)}, u32[]{:S(2)}, u32[]{:S(2)}) %collective-permute-start) | collective-permute-done | bytes 262176 | tf_op jit(solution)/shard_map/while/body/eval_jaxpr/ppermute | solution.py:10
  221.0 5.7 %psum.30 = f32[256]{0:T(256)S(1)} all-reduce(f32[256]{0:T(256)S(1)} %get-tuple-element.160), channel_id=1, replica_groups=mesh['blk'=8,'rep'=4] {'rep'}, use_global_device_ids=true, to_apply=%region_6.7 | all-reduce | flops 256 | bytes 2048 | tf_op jit(solution)/shard_map/psum | solution.py:51
  226.8 17.1 %psum.31 = f32[256]{0:T(256)S(1)} all-reduce(f32[256]{0:T(256)S(1)} %psum.30), channel_id=1, replica_groups=mesh['blk'=8,'rep'=4] {'blk'}, use_global_device_ids=true, to_apply=%region_7.8 | all-reduce | flops 256 | bytes 2048 | tf_op jit(solution)/shard_map/psum | solution.py:51
  244.4 1.7 broadcast_multiply_fusion
  (70 shorter events, 6.4 us)
Async XLA Ops:
  7.2 55.8 %copy-start = (bf16[1,16,128,128]{3,2,1,0:T(8,128)(2,1)S(1)}, bf16[1,16,128,128]{3,2,1,0:T(8,128)(2,1)}, u32[]{:S(2)}) copy-start(bf16[1,16,128,128]{3,2,1,0:T(8,128)(2,1)} %param.11) | copy-start | bytes 1572868
  7.2 46.0 %all-gather.2.cloned.1.call-start = ((), (), s32[]{:S(2)}) async-start(), calls=%async_computation.1 | async-start | bytes 1179648 | tf_op jit(solution)/shard_map/all_gather | solution.py:27
  7.9 87.2 %reduce-scatter.2.cloned.1.call-start = ((), (), s32[]{:S(2)}) async-start(), calls=%async_computation.2 | async-start | bytes 1310720 | tf_op jit(solution)/shard_map/reduce_scatter | solution.py:40
  65.3 2.1 copy-start.4
  70.1 25.0 %copy-start.2 = (bf16[256,256]{1,0:T(8,128)(2,1)S(1)}, bf16[256,256]{1,0:T(8,128)(2,1)}, u32[]{:S(2)}) copy-start(bf16[256,256]{1,0:T(8,128)(2,1)} %param.15) | copy-start | bytes 393220
  70.1 25.0 %copy-start.5 = (bf16[256,256]{1,0:T(8,128)(2,1)S(1)}, bf16[256,256]{1,0:T(8,128)(2,1)}, u32[]{:S(2)}) copy-start(bf16[256,256]{1,0:T(8,128)(2,1)} %param.17) | copy-start | bytes 393220
  70.1 25.0 %copy-start.6 = (f32[256]{0:T(256)S(1)}, f32[256]{0:T(256)}, u32[]{:S(2)}) copy-start(f32[256]{0:T(256)} %param.16) | copy-start | bytes 3076
  71.4 59.3 %all-reduce.3.cloned.1.call-start = ((), (), s32[]{:S(2)}) async-start(), calls=%async_computation.3 | async-start | bytes 524288 | tf_op jit(solution)/shard_map/psum | solution.py:51
  95.1 2.2 copy-start.1
  98.3 146.2 %all-reduce.5.cloned.1.call-start = ((), (), s32[]{:S(2)}) async-start(), calls=%async_computation.4 | async-start | bytes 524288 | tf_op jit(solution)/shard_map/psum | solution.py:51
  107.5 23.3 %copy-start.3 = (s32[1,16]{1,0:T(1,128)S(1)}, s32[1,16]{1,0:T(1,128)}, u32[]{:S(2)}) copy-start(s32[1,16]{1,0:T(1,128)} %param.13) | copy-start | bytes 196
  131.7 9.4 %collective-permute-start = (f32[256,256]{1,0:T(8,128)S(1)}, f32[256,256]{1,0:T(8,128)S(1)}, u32[]{:S(2)}, u32[]{:S(2)}) collective-permute-start(f32[256,256]{1,0:T(8,128)S(1)} %bitcast_add_fusion.2), channel_id=1, source_target_pairs={{28,0},{0,4},{4,8},{8,12},{12,16},{16,20},{20,24},{24,28},{29,1},{... | collective-permute-start | bytes 786440 | tf_op jit(solution)/shard_map/while/body/eval_jaxpr/ppermute | solution.py:10
  142.1 10.6 %collective-permute-start = (f32[256,256]{1,0:T(8,128)S(1)}, f32[256,256]{1,0:T(8,128)S(1)}, u32[]{:S(2)}, u32[]{:S(2)}) collective-permute-start(f32[256,256]{1,0:T(8,128)S(1)} %bitcast_add_fusion.2), channel_id=1, source_target_pairs={{28,0},{0,4},{4,8},{8,12},{12,16},{16,20},{20,24},{24,28},{29,1},{... | collective-permute-start | bytes 786440 | tf_op jit(solution)/shard_map/while/body/eval_jaxpr/ppermute | solution.py:10
  153.6 9.4 %collective-permute-start = (f32[256,256]{1,0:T(8,128)S(1)}, f32[256,256]{1,0:T(8,128)S(1)}, u32[]{:S(2)}, u32[]{:S(2)}) collective-permute-start(f32[256,256]{1,0:T(8,128)S(1)} %bitcast_add_fusion.2), channel_id=1, source_target_pairs={{28,0},{0,4},{4,8},{8,12},{12,16},{16,20},{20,24},{24,28},{29,1},{... | collective-permute-start | bytes 786440 | tf_op jit(solution)/shard_map/while/body/eval_jaxpr/ppermute | solution.py:10
  163.9 9.2 %collective-permute-start = (f32[256,256]{1,0:T(8,128)S(1)}, f32[256,256]{1,0:T(8,128)S(1)}, u32[]{:S(2)}, u32[]{:S(2)}) collective-permute-start(f32[256,256]{1,0:T(8,128)S(1)} %bitcast_add_fusion.2), channel_id=1, source_target_pairs={{28,0},{0,4},{4,8},{8,12},{12,16},{16,20},{20,24},{24,28},{29,1},{... | collective-permute-start | bytes 786440 | tf_op jit(solution)/shard_map/while/body/eval_jaxpr/ppermute | solution.py:10
  174.0 10.0 %collective-permute-start = (f32[256,256]{1,0:T(8,128)S(1)}, f32[256,256]{1,0:T(8,128)S(1)}, u32[]{:S(2)}, u32[]{:S(2)}) collective-permute-start(f32[256,256]{1,0:T(8,128)S(1)} %bitcast_add_fusion.2), channel_id=1, source_target_pairs={{28,0},{0,4},{4,8},{8,12},{12,16},{16,20},{20,24},{24,28},{29,1},{... | collective-permute-start | bytes 786440 | tf_op jit(solution)/shard_map/while/body/eval_jaxpr/ppermute | solution.py:10
  184.9 10.5 %collective-permute-start = (f32[256,256]{1,0:T(8,128)S(1)}, f32[256,256]{1,0:T(8,128)S(1)}, u32[]{:S(2)}, u32[]{:S(2)}) collective-permute-start(f32[256,256]{1,0:T(8,128)S(1)} %bitcast_add_fusion.2), channel_id=1, source_target_pairs={{28,0},{0,4},{4,8},{8,12},{12,16},{16,20},{20,24},{24,28},{29,1},{... | collective-permute-start | bytes 786440 | tf_op jit(solution)/shard_map/while/body/eval_jaxpr/ppermute | solution.py:10
  196.3 14.0 %collective-permute-start = (f32[256,256]{1,0:T(8,128)S(1)}, f32[256,256]{1,0:T(8,128)S(1)}, u32[]{:S(2)}, u32[]{:S(2)}) collective-permute-start(f32[256,256]{1,0:T(8,128)S(1)} %bitcast_add_fusion.2), channel_id=1, source_target_pairs={{28,0},{0,4},{4,8},{8,12},{12,16},{16,20},{20,24},{24,28},{29,1},{... | collective-permute-start | bytes 786440 | tf_op jit(solution)/shard_map/while/body/eval_jaxpr/ppermute | solution.py:10
  211.2 9.1 %collective-permute-start = (f32[256,256]{1,0:T(8,128)S(1)}, f32[256,256]{1,0:T(8,128)S(1)}, u32[]{:S(2)}, u32[]{:S(2)}) collective-permute-start(f32[256,256]{1,0:T(8,128)S(1)} %bitcast_add_fusion.2), channel_id=1, source_target_pairs={{28,0},{0,4},{4,8},{8,12},{12,16},{16,20},{20,24},{24,28},{29,1},{... | collective-permute-start | bytes 786440 | tf_op jit(solution)/shard_map/while/body/eval_jaxpr/ppermute | solution.py:10
Sparse Core Ops, SparseCore 0:
  10.1 42.9 all-gather.1
  71.6 23.4 reduce-scatter.1
  98.4 32.2 all-reduce.2
  133.9 75.5 all-reduce.4
